TPU v7x, 128 devices: a whole 4x4x4 slice. The times are simulated.
128 devices in a mesh: bx: 32 (over x, z, core), by: 2 (over y_hi), col: 2 (over y_lo).
Axes of the slice: x: 4, y: 4 (y_hi: 2, y_lo: 2; y = y_hi * 2 + y_lo), z: 4, core: 2. Of those that a mesh axis runs over, the one named last changes fastest.
Arguments:
- multipoles: bfloat16 [2, 152, 32, 1024], P(None, 'col', 'bx', 'by'), may hold values from -6 to 6
- kernel: bfloat16 [2, 32, 32, 17, 152, 152], P(None, 'bx', 'by', None, 'col'), may hold values from -0.5 to 0.5
Outputs:
- locals_out: float32 [2, 152, 32, 1024], P(None, 'col', 'bx', 'by')
All inputs are finite; a program needn't handle non-finite values.
Results may differ from a plain program's by a relative error of at most 0.0029.
Values may be sent and summed in bfloat16 or wider, within the bound.
No kernel may reach another device: no remote copies, remote signals or barrier semaphores. Data moves between devices by JAX's collectives and lax.ppermute only.
A program may use at most 128 MiB of HBM per device.

v0:
```python
import math
import jax
import jax.numpy as jnp
from jax import lax
from jax.sharding import PartitionSpec as P

NB = 32
KZ = 17
precise = lax.Precision.HIGHEST


def angle_table(count_in, count_out):
    left_index = jnp.arange(count_in, dtype=jnp.int32)[:, None]
    second = jnp.arange(count_out, dtype=jnp.int32)[None, :]
    phases = (left_index * second % count_in).astype(jnp.float32) * (2.0 * math.pi / count_in)
    return (jnp.cos(phases), jnp.sin(phases))


def contract(pattern, values, table):
    return jnp.einsum(pattern, values, table, precision=precise)


def to_planes(spatial):
    return lax.all_to_all(
        lax.all_to_all(spatial, "bx", split_axis=4, concat_axis=2, tiled=True),
        "by",
        split_axis=0,
        concat_axis=3,
        tiled=True,
    )


def to_columns(waves):
    return lax.all_to_all(
        lax.all_to_all(waves, "bx", split_axis=3, concat_axis=5, tiled=True),
        "by",
        split_axis=4,
        concat_axis=1,
        tiled=True,
    )


def back_planes(columns):
    return lax.all_to_all(
        lax.all_to_all(columns, "bx", split_axis=5, concat_axis=3, tiled=True),
        "by",
        split_axis=1,
        concat_axis=4,
        tiled=True,
    )


def back_boxes(planes):
    return lax.all_to_all(
        lax.all_to_all(planes, "bx", split_axis=2, concat_axis=4, tiled=True),
        "by",
        split_axis=3,
        concat_axis=0,
        tiled=True,
    )


def kernel_terms(kernel_part, panel):
    pattern = "abkij,rjabk->riabk"
    real_part = jnp.einsum(
        pattern, kernel_part[0], panel[0], preferred_element_type=jnp.float32
    ) - jnp.einsum(pattern, kernel_part[1], panel[1], preferred_element_type=jnp.float32)
    imag_part = jnp.einsum(
        pattern, kernel_part[0], panel[1], preferred_element_type=jnp.float32
    ) + jnp.einsum(pattern, kernel_part[1], panel[0], preferred_element_type=jnp.float32)
    return (real_part, imag_part)


def apply_kernel(spectrum, kernel):
    panels = lax.all_gather(spectrum, "col", axis=2, tiled=True)
    return kernel_terms(kernel, panels)


def on_device(multipoles, kernel):
    rhs_count, coeffs, x_local, plane_cells = multipoles.shape
    grid_side = NB
    cos_grid, sin_grid = angle_table(grid_side, grid_side)
    cos_half, sin_half = angle_table(grid_side, KZ)
    spatial_raw = multipoles.reshape(
        rhs_count, coeffs, x_local, plane_cells // grid_side, grid_side
    )
    along_x = "rcxyz,xk->rckyz"
    along_y = "rckyz,yl->rcklz"
    planes = to_planes(spatial_raw).astype(jnp.float32)
    first_re = contract(along_x, planes, cos_grid)
    first_im = -contract(along_x, planes, sin_grid)
    wave_re = contract(along_y, first_re, cos_grid) + contract(along_y, first_im, sin_grid)
    wave_im = contract(along_y, first_im, cos_grid) - contract(along_y, first_re, sin_grid)
    columns = to_columns(jnp.stack([wave_re, wave_im]))
    along_z = "rcabz,zk->rcabk"
    spec_re = contract(along_z, columns[0], cos_half) + contract(along_z, columns[1], sin_half)
    spec_im = contract(along_z, columns[1], cos_half) - contract(along_z, columns[0], sin_half)
    spectrum = jnp.stack([spec_re, spec_im]).astype(jnp.bfloat16)
    local_re, local_im = apply_kernel(spectrum, kernel)
    freq_index = jnp.arange(KZ, dtype=jnp.int32)
    weights = jnp.where((freq_index == 0) | (freq_index == grid_side // 2), 1.0, 2.0).astype(
        jnp.float32
    )
    cos_back = cos_half * weights[None, :]
    sin_back = sin_half * weights[None, :]
    from_z = "rcabk,zk->rcabz"
    back_re = contract(from_z, local_re, cos_back) - contract(from_z, local_im, sin_back)
    back_im = contract(from_z, local_re, sin_back) + contract(from_z, local_im, cos_back)
    planes_back = back_planes(jnp.stack([back_re, back_im]))
    turn_re = contract(along_x, planes_back[0], cos_grid) - contract(
        along_x, planes_back[1], sin_grid
    )
    turn_im = contract(along_x, planes_back[0], sin_grid) + contract(
        along_x, planes_back[1], cos_grid
    )
    spatial_out = (contract(along_y, turn_re, cos_grid) - contract(along_y, turn_im, sin_grid)) * (
        1.0 / float(grid_side**3)
    )
    result = back_boxes(spatial_out)
    return result.reshape(rhs_count, coeffs, x_local, plane_cells)


def solution(mesh):
    placed = (P(None, "col", "bx", "by"), P(None, "bx", "by", None, "col", None))
    return jax.shard_map(
        on_device, mesh=mesh, in_specs=placed, out_specs=P(None, "col", "bx", "by"), check_vma=False
    )
```

profile of v0, /device:TPU:1, one launch (start us, length us, event | category | flops | bytes accessed | tf_op | source)
XLA Modules:
  0.0 250.1 jit_solution(13036597349925570126)
XLA Ops:
  0.0 1.1 copy.42
  1.2 18.2 %all_to_all.132 = bf16[2,76,1,16,32]{1,3,0,2,4:T(8,128)(2,1)S(1)} all-to-all(bf16[2,76,1,16,32]{1,3,0,2,4:T(8,128)(2,1)S(1)} %copy.43), channel_id=1, replica_groups=mesh['bx'=32,'by'=2,'col'=2] {'bx'}, dimensions={4} | all-to-all | bytes 311296 | tf_op jit(solution)/shard_map/all_to_all | solution.py:25
  19.5 10.3 %all_to_all.133 = bf16[2,76,32,16,1]{1,2,3,4,0:T(8,128)(2,1)S(1)} all-to-all(bf16[2,76,32,16,1]{1,2,3,4,0:T(8,128)(2,1)S(1)} %copy.44), channel_id=1, replica_groups=mesh['bx'=32,'by'=2,'col'=2] {'by'}, dimensions={0} | all-to-all | bytes 311296 | tf_op jit(solution)/shard_map/all_to_all | solution.py:24
  31.6 0.9 fusion.38
  32.5 0.9 fusion.16
  34.5 21.3 %all_to_all.134 = f32[2,1,76,32,32,1]{2,4,5,1,0,3:T(8,128)S(1)} all-to-all(f32[2,1,76,32,32,1]{2,4,5,1,0,3:T(8,128)S(1)} %copy.49), channel_id=1, replica_groups=mesh['bx'=32,'by'=2,'col'=2] {'bx'}, dimensions={3} | all-to-all | bytes 1245184 | tf_op jit(solution)/shard_map/all_to_all | solution.py:35
  55.8 1.6 copy.50
  57.4 3.6 %all-to-all-start.3 = ((f32[2,1,76,1,32,32]{2,5,0,3,1,4:T(8,128)}), f32[2,1,76,1,32,32]{2,5,0,3,1,4:T(8,128)S(1)}, u32[]{:S(2)}, u32[]{:S(2)}) async-start(f32[2,1,76,1,32,32]{2,5,0,3,1,4:T(8,128)} %copy.50), calls=%async_computation.3 | async-start | bytes 2097152 | tf_op jit(solution)/shard_map/all_to_all | solution.py:34
  61.0 15.2 %fusion.200 = (bf16[1,1,16,17,76,152]{5,2,4,3,1,0:T(8,128)(2,1)}, bf16[1,1,16,17,76,152]{5,2,4,3,1,0:T(8,128)(2,1)}) fusion(bf16[2,1,16,17,76,152]{5,2,4,3,1,0:T(8,128)(2,1)} %param.3), kind=kLoop, calls=%fused_computation.195 | loop fusion | bytes 25137152 | tf_op jit(solution)/shard_map/slice | solution.py:66
  76.2 18.9 %copy.73 = bf16[1,1,16,17,76,152]{4,5,3,2,1,0:T(8,128)(2,1)} copy(bf16[1,1,16,17,76,152]{5,2,4,3,1,0:T(8,128)(2,1)} %get-tuple-element.5) | data formatting | bytes 12568576
  95.1 18.8 %copy.75 = bf16[1,1,16,17,76,152]{4,5,3,2,1,0:T(8,128)(2,1)} copy(bf16[1,1,16,17,76,152]{5,2,4,3,1,0:T(8,128)(2,1)} %get-tuple-element.6) | data formatting | bytes 12568576
  116.4 2.2 copy.52
  118.6 29.5 %all_gather.3 = bf16[2,2,152,1,16,17]{5,4,3,1,0,2:T(8,128)(2,1)S(1)} all-gather(bf16[2,2,76,1,16,17]{5,4,3,1,0,2:T(8,128)(2,1)S(1)} %copy.52), channel_id=1, replica_groups=mesh['bx'=32,'by'=2,'col'=2] {'col'}, dimensions={2}, use_global_device_ids=true | all-gather | bytes 496128 | tf_op jit(solution)/shard_map/all_gather | solution.py:75
  148.5 1.4 copy.72
  149.9 1.6 copy.74
  151.5 7.1 %fusion = f32[16,17,2,76]{3,2,1,0:T(2,128)S(1)} fusion(bf16[1,1,16,17,76,152]{4,5,3,2,1,0:T(8,128)(2,1)} %copy.75, bf16[1,2,152,1,16,17]{2,1,5,4,3,0:T(2,128)(2,1)S(1)} %copy.72), kind=kOutput, calls=%fused_computation | convolution fusion | flops 12568576 | bytes 6615040 | tf_op jit(solution)/shard_map/abkij,rjabk->riabk/dot_general | solution.py:70
  158.6 7.1 %fusion.2 = f32[16,17,2,76]{3,2,1,0:T(2,128)S(1)} fusion(bf16[1,1,16,17,76,152]{4,5,3,2,1,0:T(8,128)(2,1)} %copy.75, bf16[1,2,152,1,16,17]{2,1,5,4,3,0:T(2,128)(2,1)S(1)} %copy.74), kind=kOutput, calls=%fused_computation.2 | convolution fusion | flops 12568576 | bytes 6615040 | tf_op jit(solution)/shard_map/abkij,rjabk->riabk/dot_general | solution.py:67
  165.7 3.0 %fusion.24 = f32[2,76,16,17]{1,0,3,2:T(2,128)S(1)} fusion(f32[16,17,2,76]{3,2,1,0:T(2,128)S(1)} %fusion.2, bf16[1,1,16,17,76,152]{4,5,3,2,1,0:T(8,128)(2,1)S(1)} %bitcast.198, bf16[1,2,152,1,16,17]{2,1,5,4,3,0:T(2,128)(2,1)S(1)} %copy.72), kind=kOutput, calls=%fused_computation.33 | convolution fusion | flops 12609920 | bytes 6780416 | tf_op jit(solution)/shard_map/abkij,rjabk->riabk/dot_general | solution.py:65
  170.1 3.0 %fusion.30 = f32[2,76,16,17]{1,0,3,2:T(2,128)S(1)} fusion(f32[16,17,2,76]{3,2,1,0:T(2,128)S(1)} %fusion, bf16[1,1,16,17,76,152]{4,5,3,2,1,0:T(8,128)(2,1)S(1)} %bitcast.198, bf16[1,2,152,1,16,17]{2,1,5,4,3,0:T(2,128)(2,1)S(1)} %copy.74), kind=kOutput, calls=%fused_computation.35 | convolution fusion | flops 12609920 | bytes 6780416 | tf_op jit(solution)/shard_map/abkij,rjabk->riabk/dot_general | solution.py:68
  175.4 21.2 %all_to_all.135 = f32[2,2,76,1,16,32]{2,4,1,3,0,5:T(8,128)S(1)} all-to-all(f32[2,2,76,1,16,32]{2,4,1,3,0,5:T(8,128)S(1)} %copy.61), channel_id=1, replica_groups=mesh['bx'=32,'by'=2,'col'=2] {'bx'}, dimensions={5} | all-to-all | bytes 1245184 | tf_op jit(solution)/shard_map/all_to_all | solution.py:45
  197.2 18.8 %all_to_all.136 = f32[2,2,76,32,16,1]{2,3,4,0,5,1:T(8,128)S(1)} all-to-all(f32[2,2,76,32,16,1]{2,3,4,0,5,1:T(8,128)S(1)} %copy.62), channel_id=1, replica_groups=mesh['bx'=32,'by'=2,'col'=2] {'by'}, dimensions={1} | all-to-all | bytes 1245184 | tf_op jit(solution)/shard_map/all_to_all | solution.py:44
  220.5 16.1 %all_to_all.137 = f32[1,76,32,32,1]{1,3,4,0,2:T(8,128)S(1)} all-to-all(f32[1,76,32,32,1]{1,3,4,0,2:T(8,128)S(1)} %fusion.10), channel_id=1, replica_groups=mesh['bx'=32,'by'=2,'col'=2] {'bx'}, dimensions={2} | all-to-all | bytes 622592 | tf_op jit(solution)/shard_map/all_to_all | solution.py:55
  236.9 12.3 %all_to_all.138 = f32[1,76,1,32,32]{1,4,2,0,3:T(8,128)S(1)} all-to-all(f32[1,76,1,32,32]{1,4,2,0,3:T(8,128)S(1)} %copy.66), channel_id=1, replica_groups=mesh['bx'=32,'by'=2,'col'=2] {'by'}, dimensions={3} | all-to-all | bytes 622592 | tf_op jit(solution)/shard_map/all_to_all | solution.py:54
  249.2 0.9 copy.67
  (39 shorter events, 14.9 us)
Async XLA Ops:
  57.4 56.5 %all-to-all-start.3 = ((f32[2,1,76,1,32,32]{2,5,0,3,1,4:T(8,128)}), f32[2,1,76,1,32,32]{2,5,0,3,1,4:T(8,128)S(1)}, u32[]{:S(2)}, u32[]{:S(2)}) async-start(f32[2,1,76,1,32,32]{2,5,0,3,1,4:T(8,128)} %copy.50), calls=%async_computation.3 | async-start | bytes 2097152 | tf_op jit(solution)/shard_map/all_to_all | solution.py:34
  151.5 14.2 %slice-start = ((s8[10584064]{0:T(1024)(128)(4,1)}), s8[4194304]{0:T(1024)(128)(4,1)S(1)}, s32[]{:S(2)}) async-start(s8[10584064]{0:T(1024)(128)(4,1)} %bitcast.197), calls=%async_computation.8 | async-start | bytes 8388608
  151.5 14.2 %slice-start.1 = ((s8[10584064]{0:T(1024)(128)(4,1)}), s8[4194304]{0:T(1024)(128)(4,1)S(1)}, s32[]{:S(2)}) async-start(s8[10584064]{0:T(1024)(128)(4,1)} %bitcast.197), calls=%async_computation.9 | async-start | bytes 8388608
  158.6 7.1 %slice-start.2 = ((s8[10584064]{0:T(1024)(128)(4,1)}), s8[2195456]{0:T(1024)(128)(4,1)S(1)}, s32[]{:S(2)}) async-start(s8[10584064]{0:T(1024)(128)(4,1)} %bitcast.197), calls=%async_computation.10 | async-start | bytes 4390912
where the time goes:
time: 251 us; the launch traced here: 250 us
  blocking collectives  148 us (59%)
  local copies, waits for them, and re-layouts  64.4 us (26%)
  matrix products  33.9 us (14%)
  starting transfers between devices  3.58 us (1%)
    unnamed x11, local copies, waits for them, and re-layouts  41.8 us
    all_gather x1, blocking collectives, apply_kernel(): panels = lax.all_gather(spectrum, 'col', axis=2, tiled=True)  29.5 us
    all_to_all x1, blocking collectives, to_columns(): lax.all_to_all(waves, 'bx', split_axis=3, concat_axis=5, tiled=True)  21.3 us
    all_to_all x1, blocking collectives, back_planes(): lax.all_to_all(columns, 'bx', split_axis=5, concat_axis=3, tiled=True)  21.2 us
    all_to_all x1, blocking collectives, back_planes(): lax.all_to_all(lax.all_to_all(columns, 'bx', split_axis=5, concat_axis=3,...  18.8 us
    all_to_all x1, blocking collectives, to_planes(): lax.all_to_all(spatial, 'bx', split_axis=4, concat_axis=2, tiled=True)  18.2 us
    all_to_all x1, blocking collectives, back_boxes(): lax.all_to_all(planes, 'bx', split_axis=2, concat_axis=4, tiled=True)  16.1 us
    slice x1, local copies, waits for them, and re-layouts, kernel_terms(): kernel_part[0]  15.2 us
  transfers between devices with their start and end apart: 1, of which 0 were waited for; matrix products, arithmetic and copies ran while one was open for 21% of the time, Pallas kernels for 0%

commit v1 on v0

--- a/solution.py
+++ b/solution.py
@@ -72,7 +72,8 @@
 
 
 def apply_kernel(spectrum, kernel):
-    panels = lax.all_gather(spectrum, "col", axis=2, tiled=True)
+    outgoing = jnp.stack([spectrum] * lax.axis_size("col"))
+    panels = jnp.concatenate(lax.all_to_all(outgoing, "col", 0, 0), axis=2)
     return kernel_terms(kernel, panels)
 
 

time: 251 us -> 229 us (0.912)
  blocking collectives: 148 us -> 134 us
  local copies, waits for them, and re-layouts: 64.4 us -> 59.8 us
  matrix products: 33.9 us -> 30 us
    all_gather x1 -> x0, blocking collectives: 29.5 us -> none  [apply_kernel(): panels = lax.all_gather(spectrum, 'col', axis=2, tiled=True)]
    all_to_all x0 -> x1, blocking collectives: none -> 17.5 us  [to_columns(): lax.all_to_all(lax.all_to_all(waves, 'bx', split_axis=3, concat_axis=5, t...]
    dot_general x1, matrix products: 7.08 us -> 2.93 us  [kernel_terms(): jnp.einsum(pattern, kernel_part[1], panel[1], preferred_element_type=jnp....]
    unnamed x11, local copies, waits for them, and re-layouts: 41.8 us -> 39.1 us
  transfers between devices with their start and end apart: 1 -> 1, of which waited for: 0 -> 0; matrix products, arithmetic and copies ran while one was open for 21% -> 23% of each run, Pallas kernels for 0% -> 0%
where the time goes in v1:
time: 229 us; the launch traced here: 228 us
  blocking collectives  134 us (59%)
  local copies, waits for them, and re-layouts  59.8 us (26%)
  matrix products  30 us (13%)
  starting transfers between devices  3.49 us (2%)
    unnamed x11, local copies, waits for them, and re-layouts  39.1 us
    all_to_all x1, blocking collectives, to_columns(): lax.all_to_all(waves, 'bx', split_axis=3, concat_axis=5, tiled=True)  21.3 us
    all_to_all x1, blocking collectives, back_planes(): lax.all_to_all(columns, 'bx', split_axis=5, concat_axis=3, tiled=True)  21.2 us
    all_to_all x1, blocking collectives, to_planes(): lax.all_to_all(spatial, 'bx', split_axis=4, concat_axis=2, tiled=True)  18.2 us
    all_to_all x1, blocking collectives, to_columns(): lax.all_to_all(lax.all_to_all(waves, 'bx', split_axis=3, concat_axis=5, t...  17.5 us
    all_to_all x1, blocking collectives, back_planes(): lax.all_to_all(lax.all_to_all(columns, 'bx', split_axis=5, concat_axis=3,...  17.5 us
    all_to_all x1, blocking collectives, back_boxes(): lax.all_to_all(planes, 'bx', split_axis=2, concat_axis=4, tiled=True)  15.9 us
    slice x1, local copies, waits for them, and re-layouts, kernel_terms(): kernel_part[0]  15.2 us
  transfers between devices with their start and end apart: 1, of which 0 were waited for; matrix products, arithmetic and copies ran while one was open for 23% of the time, Pallas kernels for 0%

profile of v1, /device:TPU:1, one launch (start us, length us, event | category | flops | bytes accessed | tf_op | source)
XLA Modules:
  0.0 228.1 jit_solution(10128571044007991757)
XLA Ops:
  0.0 1.1 copy.40
  1.2 18.2 %all_to_all.137 = bf16[2,76,1,16,32]{1,3,0,2,4:T(8,128)(2,1)S(1)} all-to-all(bf16[2,76,1,16,32]{1,3,0,2,4:T(8,128)(2,1)S(1)} %copy.41), channel_id=1, replica_groups=mesh['bx'=32,'by'=2,'col'=2] {'bx'}, dimensions={4} | all-to-all | bytes 311296 | tf_op jit(solution)/shard_map/all_to_all | solution.py:25
  19.5 10.3 %all_to_all.138 = bf16[2,76,32,16,1]{1,2,3,4,0:T(8,128)(2,1)S(1)} all-to-all(bf16[2,76,32,16,1]{1,2,3,4,0:T(8,128)(2,1)S(1)} %copy.42), channel_id=1, replica_groups=mesh['bx'=32,'by'=2,'col'=2] {'by'}, dimensions={0} | all-to-all | bytes 311296 | tf_op jit(solution)/shard_map/all_to_all | solution.py:24
  31.6 0.9 fusion.38
  32.5 0.9 fusion.16
  33.4 0.9 fusion.15
  34.5 21.3 %all_to_all.139 = f32[2,1,76,32,32,1]{2,4,5,1,0,3:T(8,128)S(1)} all-to-all(f32[2,1,76,32,32,1]{2,4,5,1,0,3:T(8,128)S(1)} %copy.47), channel_id=1, replica_groups=mesh['bx'=32,'by'=2,'col'=2] {'bx'}, dimensions={3} | all-to-all | bytes 1245184 | tf_op jit(solution)/shard_map/all_to_all | solution.py:35
  56.4 17.5 %all_to_all.140 = f32[2,1,76,1,32,32]{2,5,0,3,1,4:T(8,128)S(1)} all-to-all(f32[2,1,76,1,32,32]{2,5,0,3,1,4:T(8,128)S(1)} %copy.48), channel_id=1, replica_groups=mesh['bx'=32,'by'=2,'col'=2] {'by'}, dimensions={4} | all-to-all | bytes 1245184 | tf_op jit(solution)/shard_map/all_to_all | solution.py:34
  76.5 0.9 copy.50
  77.4 3.5 %all-to-all-start.4 = ((bf16[2,2,2,76,1,16,17]{3,5,6,4,2,1,0:T(8,128)(2,1)}), bf16[2,2,2,76,1,16,17]{3,5,6,4,2,1,0:T(8,128)(2,1)S(1)}, u32[]{:S(2)}, u32[]{:S(2)}) async-start(bf16[2,2,2,76,1,16,17]{3,5,6,4,2,1,0:T(8,128)(2,1)} %copy.50), calls=%async_computation.4 | async-start | bytes 1114112 | tf_op jit(solution)/shard_map/all_to_all | solution.py:76
  80.9 15.2 %fusion.196 = (bf16[1,1,16,17,76,152]{5,2,4,3,1,0:T(8,128)(2,1)}, bf16[1,1,16,17,76,152]{5,2,4,3,1,0:T(8,128)(2,1)}) fusion(bf16[2,1,16,17,76,152]{5,2,4,3,1,0:T(8,128)(2,1)} %param.3), kind=kLoop, calls=%fused_computation.191 | loop fusion | bytes 25137152 | tf_op jit(solution)/shard_map/slice | solution.py:66
  96.0 18.8 %copy.78 = bf16[1,1,16,17,76,152]{4,5,3,2,1,0:T(8,128)(2,1)} copy(bf16[1,1,16,17,76,152]{5,2,4,3,1,0:T(8,128)(2,1)} %get-tuple-element.5) | data formatting | bytes 12568576
  114.9 18.8 %copy.79 = bf16[1,1,16,17,76,152]{4,5,3,2,1,0:T(8,128)(2,1)} copy(bf16[1,1,16,17,76,152]{5,2,4,3,1,0:T(8,128)(2,1)} %get-tuple-element.6) | data formatting | bytes 12568576
  135.0 7.1 %fusion = f32[16,17,2,76]{3,2,1,0:T(2,128)S(1)} fusion(bf16[2,152,16,17]{1,0,3,2:T(2,128)(2,1)S(1)} %reshape.215, bf16[1,1,16,17,76,152]{4,5,3,2,1,0:T(8,128)(2,1)} %copy.79), kind=kOutput, calls=%fused_computation | convolution fusion | flops 12568576 | bytes 6615040 | tf_op jit(solution)/shard_map/abkij,rjabk->riabk/dot_general | solution.py:70
  142.0 2.9 %fusion.2 = f32[16,17,2,76]{3,2,1,0:T(2,128)S(1)} fusion(bf16[2,152,16,17]{1,0,3,2:T(2,128)(2,1)S(1)} %reshape.216, bf16[1,1,16,17,76,152]{4,5,3,2,1,0:T(8,128)(2,1)S(1)} %copy-done), kind=kOutput, calls=%fused_computation.2 | convolution fusion | flops 12568576 | bytes 6615040 | tf_op jit(solution)/shard_map/abkij,rjabk->riabk/dot_general | solution.py:67
  145.2 3.0 %fusion.24 = f32[2,76,16,17]{1,0,3,2:T(2,128)S(1)} fusion(f32[16,17,2,76]{3,2,1,0:T(2,128)S(1)} %fusion.2, bf16[2,152,16,17]{1,0,3,2:T(2,128)(2,1)S(1)} %reshape.215, bf16[1,1,16,17,76,152]{4,5,3,2,1,0:T(8,128)(2,1)S(1)} %bitcast.197), kind=kOutput, calls=%fused_computation.33 | convolution fusion | flops 12609920 | bytes 6780416 | tf_op jit(solution)/shard_map/abkij,rjabk->riabk/dot_general | solution.py:65
  149.6 3.0 %fusion.30 = f32[2,76,16,17]{1,0,3,2:T(2,128)S(1)} fusion(f32[16,17,2,76]{3,2,1,0:T(2,128)S(1)} %fusion, bf16[2,152,16,17]{1,0,3,2:T(2,128)(2,1)S(1)} %reshape.216, bf16[1,1,16,17,76,152]{4,5,3,2,1,0:T(8,128)(2,1)S(1)} %bitcast.197), kind=kOutput, calls=%fused_computation.35 | convolution fusion | flops 12609920 | bytes 6780416 | tf_op jit(solution)/shard_map/abkij,rjabk->riabk/dot_general | solution.py:68
  153.3 0.9 fusion.14
  154.9 21.2 %all_to_all.141 = f32[2,2,76,1,16,32]{2,4,1,3,0,5:T(8,128)S(1)} all-to-all(f32[2,2,76,1,16,32]{2,4,1,3,0,5:T(8,128)S(1)} %copy.63), channel_id=1, replica_groups=mesh['bx'=32,'by'=2,'col'=2] {'bx'}, dimensions={5} | all-to-all | bytes 1245184 | tf_op jit(solution)/shard_map/all_to_all | solution.py:45
  176.7 17.5 %all_to_all.142 = f32[2,2,76,32,16,1]{2,3,4,0,5,1:T(8,128)S(1)} all-to-all(f32[2,2,76,32,16,1]{2,3,4,0,5,1:T(8,128)S(1)} %copy.64), channel_id=1, replica_groups=mesh['bx'=32,'by'=2,'col'=2] {'by'}, dimensions={1} | all-to-all | bytes 1245184 | tf_op jit(solution)/shard_map/all_to_all | solution.py:44
  197.9 0.9 fusion.10
  198.8 15.9 %all_to_all.143 = f32[1,76,32,32,1]{1,3,4,0,2:T(8,128)S(1)} all-to-all(f32[1,76,32,32,1]{1,3,4,0,2:T(8,128)S(1)} %fusion.10), channel_id=1, replica_groups=mesh['bx'=32,'by'=2,'col'=2] {'bx'}, dimensions={2} | all-to-all | bytes 622592 | tf_op jit(solution)/shard_map/all_to_all | solution.py:55
  214.9 12.3 %all_to_all.144 = f32[1,76,1,32,32]{1,4,2,0,3:T(8,128)S(1)} all-to-all(f32[1,76,1,32,32]{1,4,2,0,3:T(8,128)S(1)} %copy.68), channel_id=1, replica_groups=mesh['bx'=32,'by'=2,'col'=2] {'by'}, dimensions={3} | all-to-all | bytes 622592 | tf_op jit(solution)/shard_map/all_to_all | solution.py:54
  227.2 0.9 copy.69
  (43 shorter events, 13.9 us)
Async XLA Ops:
  77.4 56.4 %all-to-all-start.4 = ((bf16[2,2,2,76,1,16,17]{3,5,6,4,2,1,0:T(8,128)(2,1)}), bf16[2,2,2,76,1,16,17]{3,5,6,4,2,1,0:T(8,128)(2,1)S(1)}, u32[]{:S(2)}, u32[]{:S(2)}) async-start(bf16[2,2,2,76,1,16,17]{3,5,6,4,2,1,0:T(8,128)(2,1)} %copy.50), calls=%async_computation.4 | async-start | bytes 1114112 | tf_op jit(solution)/shard_map/all_to_all | solution.py:76
  134.9 7.1 %copy-start = (bf16[1,1,16,17,76,152]{4,5,3,2,1,0:T(8,128)(2,1)S(1)}, bf16[1,1,16,17,76,152]{4,5,3,2,1,0:T(8,128)(2,1)}, u32[]{:S(2)}) copy-start(bf16[1,1,16,17,76,152]{4,5,3,2,1,0:T(8,128)(2,1)} %copy.79) | copy-start | bytes 18852868
  134.9 10.0 %slice-start = ((s8[10584064]{0:T(1024)(128)(4,1)}), s8[4194304]{0:T(1024)(128)(4,1)S(1)}, s32[]{:S(2)}) async-start(s8[10584064]{0:T(1024)(128)(4,1)} %bitcast.196), calls=%async_computation.9 | async-start | bytes 8388608
  135.0 10.0 %slice-start.1 = ((s8[10584064]{0:T(1024)(128)(4,1)}), s8[4194304]{0:T(1024)(128)(4,1)S(1)}, s32[]{:S(2)}) async-start(s8[10584064]{0:T(1024)(128)(4,1)} %bitcast.196), calls=%async_computation.10 | async-start | bytes 8388608
  142.0 3.2 %slice-start.2 = ((s8[10584064]{0:T(1024)(128)(4,1)}), s8[2195456]{0:T(1024)(128)(4,1)S(1)}, s32[]{:S(2)}) async-start(s8[10584064]{0:T(1024)(128)(4,1)} %bitcast.196), calls=%async_computation.11 | async-start | bytes 4390912
